TPU v7x, 32 devices: a whole 2x2x4 slice. The times are simulated.
32 devices in a mesh: sector: 16 (over z, y, x), op: 2 (over core).
Axes of the slice: x: 2, y: 2, z: 4, core: 2. Of those that a mesh axis runs over, the one named last changes fastest.
Arguments:
- psi: bfloat16 [1024, 128, 128], P('sector'), may hold values from -6 to 6
- left_env: bfloat16 [2, 128, 128, 128], P('op', 'sector'), may hold values from -0.5 to 0.5
- right_env: bfloat16 [2, 128, 128, 128], P('op', 'sector'), may hold values from -0.375 to 0.375
- left_dims: int32 [128], replicated, may hold values from 64 to 128
- right_dims: int32 [128], replicated, may hold values from 64 to 128
- block_right: int32 [1024], replicated, may hold values from 0 to 127, as said below
Outputs:
- h_psi: bfloat16 [1024, 128, 128], P('sector', 'op')
Inputs may be any that keep to these rules, and one draw needn't show every extreme that they name: Block d * 64 + j lies in left sector d * 8 + j // 8; its right sector is owned by index block_right // 8 of sector, and block_right % 8 equals j // 8. Of the 64 blocks of each index of sector, exactly 4 have their right sector owned by each index of sector; the 8 blocks of one left sector have distinct right sectors, and every right sector is paired with exactly 8 blocks.
All inputs are finite; a program needn't handle non-finite values.
Results may differ from a plain program's by a relative error of at most 0.0049.
Values may be sent and summed in bfloat16 or wider, within the bound.
A program may use at most 64 MiB of HBM per device.

v0:
```python
import jax
import jax.numpy as jnp
from jax import lax
from jax.sharding import PartitionSpec as P


def combine(partial_sum):
    row_count = partial_sum.shape[1] // lax.axis_size("op")
    whole = lax.psum(partial_sum, "op")
    return lax.dynamic_slice_in_dim(whole, lax.axis_index("op") * row_count, row_count, 1)


def per_device(psi, left_env, right_env, left_dims, right_dims, block_right):
    devices = lax.axis_size("sector")
    sector_index = lax.axis_index("sector")
    blocks = psi.shape[0]
    block_width = psi.shape[1]
    term_count = left_env.shape[0]
    sectors = left_env.shape[1]
    coupled = blocks // sectors
    slot_count = blocks // devices
    counter = jnp.arange(blocks, dtype=jnp.int32)
    mine_right = lax.dynamic_slice_in_dim(block_right, sector_index * blocks, blocks)
    mine_owner = mine_right // sectors
    send_order = jnp.argsort(mine_owner * blocks + counter)
    inverse = jnp.argsort(send_order)
    own_dims = lax.dynamic_slice_in_dim(left_dims, sector_index * sectors, sectors)
    row_limit = jnp.repeat(own_dims, coupled)
    col_limit = right_dims[mine_right]
    position = jnp.arange(block_width, dtype=jnp.int32)
    keep_mask = (position[None, :, None] < row_limit[:, None, None]) & (
        position[None, None, :] < col_limit[:, None, None]
    )
    masked = psi * keep_mask.astype(psi.dtype)
    products = jnp.einsum(
        "ksab,snbc->ksnac",
        left_env,
        masked.reshape(sectors, coupled, block_width, block_width),
        preferred_element_type=jnp.float32,
    )
    products = products.astype(jnp.bfloat16).reshape(term_count, blocks, block_width, block_width)
    owners_all = (block_right // sectors).reshape(devices, blocks)
    foreign = (owners_all != sector_index).astype(jnp.int32)
    incoming = jnp.argsort(foreign * blocks + counter[None, :], axis=1)[:, :slot_count]
    arriving = (
        jnp.take_along_axis(block_right.reshape(devices, blocks), incoming, axis=1).reshape(-1)
        - sector_index * sectors
    )
    outgoing = right_env[:, arriving].reshape(
        term_count, devices, slot_count, block_width, block_width
    )
    received = lax.all_to_all(outgoing, "sector", split_axis=1, concat_axis=1, tiled=True)
    chosen = received.reshape(term_count, blocks, block_width, block_width)[:, inverse]
    partial_sum = jnp.einsum("kjab,kjcb->jac", products, chosen, preferred_element_type=jnp.float32)
    result = combine(partial_sum).astype(jnp.bfloat16)
    row_count = result.shape[1]
    op_index = lax.axis_index("op")
    row_position = op_index * row_count + jnp.arange(row_count, dtype=jnp.int32)
    keep_rows = (row_position[None, :, None] < row_limit[:, None, None]) & (
        position[None, None, :] < col_limit[:, None, None]
    )
    return result * keep_rows.astype(jnp.bfloat16)


def solution(mesh):
    in_specs = (
        P("sector", None, None),
        P("op", "sector", None, None),
        P("op", "sector", None, None),
        P(),
        P(),
        P(),
    )
    out_specs = P("sector", "op", None)
    return jax.shard_map(
        per_device, mesh=mesh, in_specs=in_specs, out_specs=out_specs, check_vma=False
    )
```

profile of v0, /device:TPU:13, one launch (start us, length us, event | category | flops | bytes accessed | tf_op | source)
XLA Modules:
  0.0 86.6 jit_solution(15736413275250530421)
XLA Ops:
  0.0 0.0 copy-start
  0.0 0.8 reshape.167
  0.8 0.7 fusion.4
  1.5 0.1 mul.34
  1.6 0.1 copy.23
  1.7 1.0 %sort.48 = (s32[16,64]{0,1:T(8,128)}, s32[16,64]{0,1:T(8,128)S(1)}) sort(s32[16,64]{0,1:T(8,128)S(1)} %iota_add_fusion, s32[16,64]{0,1:T(8,128)S(1)} %iota.41), dimensions={1}, to_apply=%region_0.1 | sort | flops 10240 | bytes 16384 | tf_op jit(solution)/shard_map/jit(argsort)/sort | solution.py:44
  2.7 0.1 copy.24
  2.8 0.1 reshape.200
  2.9 0.8 gather_fusion.3
  3.7 0.1 reshape.203
  3.8 0.1 copy.25
  3.9 0.1 copy.26
  4.0 0.1 sub.31
  4.1 0.0 copy-done
  4.1 2.2 %gather_fusion.1 = bf16[64,128,128]{2,1,0:T(8,128)(2,1)} fusion(bf16[8,128,128]{2,1,0:T(8,128)(2,1)S(1)} %bitcast.24, s32[1024]{0:T(1024)S(1)} %pad_clamp_fusion.1), kind=kCustom, calls=%fused_computation.1 | custom fusion | bytes 4194560 | tf_op jit(solution)/shard_map/gather | solution.py:49
  6.3 0.0 copy-start.3
  6.3 0.0 copy-start.1
  6.3 6.7 %all-to-all-start = ((bf16[1,16,4,128,128]{4,3,2,0,1:T(8,128)(2,1)}), bf16[1,16,4,128,128]{4,3,2,0,1:T(8,128)(2,1)S(1)}, u32[]{:S(2)}, u32[]{:S(2)}) async-start(bf16[1,16,4,128,128]{4,3,2,0,1:T(8,128)(2,1)} %bitcast.26), calls=%async_computation | async-start | bytes 4194304 | tf_op jit(solution)/shard_map/all_to_all | solution.py:52
  13.0 0.0 copy-done.3
  13.0 0.1 dynamic_slice.9
  13.1 0.1 broadcast_in_dim.10
  13.2 0.1 lt.98
  13.2 0.8 iota_add_fusion.1
  14.0 0.0 copy-done.1
  14.0 0.8 gather_fusion
  14.8 2.0 %sort.49 = (s32[64]{0:T(128)}, s32[64]{0:T(128)S(1)}) sort(s32[64]{0:T(128)S(1)} %get-tuple-element.11, s32[64]{0:T(128)S(1)} %iota.43), dimensions={0}, to_apply=%region_1.2 | sort | flops 384 | bytes 1024 | tf_op jit(solution)/shard_map/jit(argsort)/sort | solution.py:25
  16.9 2.0 %sort.50 = (s32[64]{0:T(128)}, s32[64]{0:T(128)S(1)}) sort(s32[64]{0:T(128)S(1)} %get-tuple-element.9, s32[64]{0:T(128)S(1)} %iota.44), dimensions={0}, to_apply=%region_2.3 | sort | flops 384 | bytes 1024 | tf_op jit(solution)/shard_map/jit(argsort)/sort | solution.py:26
  18.9 0.1 broadcast_compare_fusion
  19.0 0.1 iota_compare_fusion
  19.1 0.0 copy-start.2
  19.1 3.2 %and_select_fusion = bf16[64,128,128]{2,1,0:T(8,128)(2,1)S(1)} fusion(bf16[64,128,128]{2,1,0:T(8,128)(2,1)} %param.6, pred[64,128]{1,0:T(8,128)(4,1)S(1)} %get-tuple-element.14, pred[64,128]{1,0:T(8,128)(4,1)S(1)} %get-tuple-element.13), kind=kLoop, calls=%fused_computation.4 | loop fusion | flops 2097152 | bytes 4210688 | tf_op jit(solution)/shard_map/mul | solution.py:34
  22.3 0.0 copy-done.2
  22.3 2.1 %convolution_convert_fusion = bf16[8,8,128,128]{3,2,1,0:T(8,128)(2,1)} fusion(bf16[8,8,128,128]{3,2,1,0:T(8,128)(2,1)S(1)} %bitcast.27, bf16[1,8,128,128]{3,2,1,0:T(8,128)(2,1)S(1)} %copy-done.2), kind=kOutput, calls=%fused_computation.7 | convolution fusion | flops 269484032 | bytes 4456448 | tf_op jit(solution)/shard_map/ksab,snbc->ksnac/dot_general | solution.py:35
  24.5 36.5 %all-to-all-done = bf16[1,16,4,128,128]{4,3,2,0,1:T(8,128)(2,1)S(1)} async-done(((bf16[1,16,4,128,128]{4,3,2,0,1:T(8,128)(2,1)}), bf16[1,16,4,128,128]{4,3,2,0,1:T(8,128)(2,1)S(1)}, u32[]{:S(2)}, u32[]{:S(2)}) %all-to-all-start) | async-done | bytes 2097184 | tf_op jit(solution)/shard_map/all_to_all | solution.py:52
  61.0 2.2 %gather_fusion.2 = bf16[64,128,128]{2,1,0:T(8,128)(2,1)} fusion(bf16[64,128,128]{2,1,0:T(8,128)(2,1)S(1)} %bitcast.25, s32[1024]{0:T(1024)S(1)} %pad_clamp_fusion), kind=kCustom, calls=%fused_computation.2 | custom fusion | bytes 4194560 | tf_op jit(solution)/shard_map/gather | solution.py:53
  63.1 5.8 %fusion.6 = f32[64,128,128]{2,1,0:T(8,128)} fusion(bf16[64,128,128]{1,2,0:T(8,128)(2,1)} %bitcast.28, bf16[64,128,128]{2,1,0:T(8,128)(2,1)} %gather_fusion.2), kind=kOutput, calls=%fused_computation.38 | convolution fusion | flops 268435456 | bytes 8388608 | tf_op jit(solution)/shard_map/kjab,kjcb->jac/dot_general | solution.py:54
  68.9 16.2 %all-reduce.1 = bf16[64,128,128]{2,1,0:T(8,128)(2,1)S(1)} all-reduce(f32[64,128,128]{2,1,0:T(8,128)} %fusion.6), channel_id=1, replica_groups=mesh['sector'=16,'op'=2] {'op'}, use_global_device_ids=true, to_apply=%region_3.4 | all-reduce | flops 1048576 | bytes 6291456 | tf_op jit(solution)/shard_map/psum | solution.py:9
  85.1 1.5 %and_select_fusion.1 = bf16[64,64,128]{2,1,0:T(8,128)(2,1)} fusion(bf16[64,128,128]{2,1,0:T(8,128)(2,1)S(1)} %all-reduce.1, s32[]{:T(128)S(6)} %select_n.61, pred[64,128]{1,0:T(8,128)(4,1)S(1)} %get-tuple-element.14, pred[64,64]{1,0:T(8,128)(4,1)S(1)} %broadcast_compare_fusion), kind=kLoop, calls=%fused_computation.6 | loop fusion | flops 1048576 | bytes 2109444 | tf_op jit(solution)/shard_map/mul | solution.py:62
  (12 shorter events, 0.1 us)
Async XLA Ops:
  0.0 4.1 %copy-start = (bf16[1,8,128,128]{3,2,1,0:T(8,128)(2,1)S(1)}, bf16[1,8,128,128]{3,2,1,0:T(8,128)(2,1)}, u32[]{:S(2)}) copy-start(bf16[1,8,128,128]{3,2,1,0:T(8,128)(2,1)} %param.8) | copy-start | bytes 786436
  6.3 6.7 %copy-start.3 = (s32[128]{0:T(128)S(1)}, s32[128]{0:T(128)}, u32[]{:S(2)}) copy-start(s32[128]{0:T(128)} %param.9) | copy-start | bytes 1540
  6.3 7.8 %copy-start.1 = (s32[128]{0:T(128)S(1)}, s32[128]{0:T(128)}, u32[]{:S(2)}) copy-start(s32[128]{0:T(128)} %param.10) | copy-start | bytes 1540
  6.3 54.7 %all-to-all-start = ((bf16[1,16,4,128,128]{4,3,2,0,1:T(8,128)(2,1)}), bf16[1,16,4,128,128]{4,3,2,0,1:T(8,128)(2,1)S(1)}, u32[]{:S(2)}, u32[]{:S(2)}) async-start(bf16[1,16,4,128,128]{4,3,2,0,1:T(8,128)(2,1)} %bitcast.26), calls=%async_computation | async-start | bytes 4194304 | tf_op jit(solution)/shard_map/all_to_all | solution.py:52
  19.1 3.2 %copy-start.2 = (bf16[1,8,128,128]{3,2,1,0:T(8,128)(2,1)S(1)}, bf16[1,8,128,128]{3,2,1,0:T(8,128)(2,1)}, u32[]{:S(2)}) copy-start(bf16[1,8,128,128]{3,2,1,0:T(8,128)(2,1)} %param.7) | copy-start | bytes 786436
where the time goes:
time: 86.9 us; the launch traced here: 86.6 us
  waiting for transfers between devices  36.5 us (42%)
  blocking collectives  16.2 us (19%)
  other arithmetic  11.5 us (13%)
  matrix products  7.91 us (9%)
  local copies, waits for them, and re-layouts  7.65 us (9%)
  starting transfers between devices  6.74 us (8%)
    all_to_all x1, waiting for transfers between devices, per_device(): lax.all_to_all(outgoing, 'sector', split_axis=1, concat_axis=1, tiled=True)  36.5 us
    psum x1, blocking collectives, combine(): whole = lax.psum(partial_sum, 'op')  16.2 us
    all_to_all x1, starting transfers between devices, per_device(): lax.all_to_all(outgoing, 'sector', split_axis=1, concat_axis=1, tiled=True)  6.74 us
    dot_general x1, matrix products, per_device(): jnp.einsum('kjab,kjcb->jac', products, chosen, preferred_element_type=jnp...  5.76 us
    mul x1, other arithmetic, per_device(): masked = psi * keep_mask.astype(psi.dtype)  3.23 us
    gather x1, local copies, waits for them, and re-layouts, per_device(): right_env[:, arriving]  2.17 us
    gather x1, local copies, waits for them, and re-layouts, per_device(): received.reshape(term_count, blocks, block_width, block_width)[:, inverse]  2.16 us
    dot_general x1, matrix products, per_device(): jnp.einsum('ksab,snbc->ksnac', left_env, masked.reshape(sectors, coupled,...  2.15 us
  transfers between devices with their start and end apart: 1, of which 1 were waited for; matrix products, arithmetic and copies ran while one was open for 13% of the time, Pallas kernels for 0%

commit v1 on v0

--- a/solution.py
+++ b/solution.py
@@ -6,7 +6,8 @@
 
 def combine(partial_sum):
     row_count = partial_sum.shape[1] // lax.axis_size("op")
-    whole = lax.psum(partial_sum, "op")
+    pieces = lax.all_gather(partial_sum, "op")
+    whole = jnp.sum(pieces, axis=0)
     return lax.dynamic_slice_in_dim(whole, lax.axis_index("op") * row_count, row_count, 1)
 
 

time: 86.9 us -> 110 us (1.27)
  waiting for transfers between devices: 36.5 us -> 56.7 us
  blocking collectives: 16.2 us -> 0 us
  between operations: 0.11 us -> 13.5 us
  other arithmetic: 11.5 us -> 16.2 us
    all_gather x0 -> x1, waiting for transfers between devices: none -> 20.2 us  [combine(): pieces = lax.all_gather(partial_sum, 'op')]
    psum x1 -> x0, blocking collectives: 16.2 us -> none  [combine(): whole = lax.psum(partial_sum, 'op')]
    reduce_sum x0 -> x1, other arithmetic: none -> 4.64 us  [combine(): whole = jnp.sum(pieces, axis=0)]
  transfers between devices with their start and end apart: 1 -> 2, of which waited for: 1 -> 2; matrix products, arithmetic and copies ran while one was open for 13% -> 11% of each run, Pallas kernels for 0% -> 0%
where the time goes in v1:
time: 110 us; the launch traced here: 109 us
  waiting for transfers between devices  56.7 us (52%)
  other arithmetic  16.2 us (15%)
  between operations  13.5 us (12%)
  matrix products  7.98 us (7%)
  local copies, waits for them, and re-layouts  7.55 us (7%)
  starting transfers between devices  6.78 us (6%)
    all_to_all x1, waiting for transfers between devices, per_device(): lax.all_to_all(outgoing, 'sector', split_axis=1, concat_axis=1, tiled=True)  36.5 us
    all_gather x1, waiting for transfers between devices, combine(): pieces = lax.all_gather(partial_sum, 'op')  20.2 us
    all_to_all x1, starting transfers between devices, per_device(): lax.all_to_all(outgoing, 'sector', split_axis=1, concat_axis=1, tiled=True)  6.74 us
    dot_general x1, matrix products, per_device(): jnp.einsum('kjab,kjcb->jac', products, chosen, preferred_element_type=jnp...  5.81 us
    reduce_sum x1, other arithmetic, combine(): whole = jnp.sum(pieces, axis=0)  4.64 us
    mul x1, other arithmetic, per_device(): masked = psi * keep_mask.astype(psi.dtype)  3.23 us
  transfers between devices with their start and end apart: 2, of which 2 were waited for; matrix products, arithmetic and copies ran while one was open for 11% of the time, Pallas kernels for 0%

profile of v1, /device:TPU:13, one launch (start us, length us, event | category | flops | bytes accessed | tf_op | source)
XLA Modules:
  0.0 108.7 jit_solution(3984864027287928750)
XLA Ops:
  6.5 0.0 copy-start
  6.5 0.8 reshape.167
  7.3 0.7 fusion.4
  8.0 0.1 mul.34
  8.1 0.1 copy.23
  8.2 1.0 sort.48
  9.2 0.1 copy.24
  9.3 0.1 reshape.200
  9.4 0.8 gather_fusion.3
  10.2 0.1 reshape.203
  10.3 0.1 copy.25
  10.4 0.1 copy.26
  10.5 0.1 sub.31
  10.6 0.0 copy-done
  10.6 2.1 %gather_fusion.1 = bf16[64,128,128]{2,1,0:T(8,128)(2,1)} fusion(bf16[8,128,128]{2,1,0:T(8,128)(2,1)S(1)} %bitcast.25, s32[1024]{0:T(1024)S(1)} %pad_clamp_fusion.1), kind=kCustom, calls=%fused_computation.1 | custom fusion | bytes 4194560 | tf_op jit(solution)/shard_map/gather | solution.py:50
  12.7 0.0 copy-start.3
  12.7 0.0 copy-start.1
  12.7 6.7 %all-to-all-start = ((bf16[1,16,4,128,128]{4,3,2,0,1:T(8,128)(2,1)}), bf16[1,16,4,128,128]{4,3,2,0,1:T(8,128)(2,1)S(1)}, u32[]{:S(2)}, u32[]{:S(2)}) async-start(bf16[1,16,4,128,128]{4,3,2,0,1:T(8,128)(2,1)} %bitcast.28), calls=%async_computation | async-start | bytes 4194304 | tf_op jit(solution)/shard_map/all_to_all | solution.py:53
  19.5 0.0 all-gather.3.cloned.1.call-start
  19.5 0.0 copy-done.3
  19.5 0.1 dynamic_slice.9
  19.6 0.1 broadcast_in_dim.10
  19.7 0.1 lt.98
  19.8 0.8 iota_add_fusion.1
  20.6 0.0 copy-done.1
  20.6 0.8 gather_fusion
  21.3 2.0 %sort.49 = (s32[64]{0:T(128)}, s32[64]{0:T(128)S(1)}) sort(s32[64]{0:T(128)S(1)} %get-tuple-element.11, s32[64]{0:T(128)S(1)} %iota.43), dimensions={0}, to_apply=%region_1.2 | sort | flops 384 | bytes 1024 | tf_op jit(solution)/shard_map/jit(argsort)/sort | solution.py:26
  23.4 2.0 %sort.50 = (s32[64]{0:T(128)}, s32[64]{0:T(128)S(1)}) sort(s32[64]{0:T(128)S(1)} %get-tuple-element.9, s32[64]{0:T(128)S(1)} %iota.44), dimensions={0}, to_apply=%region_2.3 | sort | flops 384 | bytes 1024 | tf_op jit(solution)/shard_map/jit(argsort)/sort | solution.py:27
  25.4 0.1 iota_compare_fusion
  25.5 0.0 copy-start.2
  25.5 3.2 %and_select_fusion = bf16[64,128,128]{2,1,0:T(8,128)(2,1)S(1)} fusion(bf16[64,128,128]{2,1,0:T(8,128)(2,1)} %param.6, pred[64,128]{1,0:T(8,128)(4,1)S(1)} %get-tuple-element.14, pred[64,128]{1,0:T(8,128)(4,1)S(1)} %get-tuple-element.13), kind=kLoop, calls=%fused_computation.4 | loop fusion | flops 2097152 | bytes 4210688 | tf_op jit(solution)/shard_map/mul | solution.py:35
  28.8 0.0 copy-done.2
  28.8 2.2 %convolution_convert_fusion = bf16[8,8,128,128]{3,2,1,0:T(8,128)(2,1)} fusion(bf16[8,8,128,128]{3,2,1,0:T(8,128)(2,1)S(1)} %bitcast.29, bf16[1,8,128,128]{3,2,1,0:T(8,128)(2,1)S(1)} %copy-done.2), kind=kOutput, calls=%fused_computation.7 | convolution fusion | flops 269484032 | bytes 4456448 | tf_op jit(solution)/shard_map/ksab,snbc->ksnac/dot_general | solution.py:36
  31.0 36.5 %all-to-all-done = bf16[1,16,4,128,128]{4,3,2,0,1:T(8,128)(2,1)S(1)} async-done(((bf16[1,16,4,128,128]{4,3,2,0,1:T(8,128)(2,1)}), bf16[1,16,4,128,128]{4,3,2,0,1:T(8,128)(2,1)S(1)}, u32[]{:S(2)}, u32[]{:S(2)}) %all-to-all-start) | async-done | bytes 2097184 | tf_op jit(solution)/shard_map/all_to_all | solution.py:53
  67.5 2.1 %gather_fusion.2 = bf16[64,128,128]{2,1,0:T(8,128)(2,1)} fusion(bf16[64,128,128]{2,1,0:T(8,128)(2,1)S(1)} %bitcast.27, s32[1024]{0:T(1024)S(1)} %pad_clamp_fusion), kind=kCustom, calls=%fused_computation.2 | custom fusion | bytes 4194560 | tf_op jit(solution)/shard_map/gather | solution.py:54
  69.6 5.8 %fusion.6 = f32[64,128,128]{2,1,0:T(8,128)} fusion(bf16[64,128,128]{1,2,0:T(8,128)(2,1)} %bitcast.30, bf16[64,128,128]{2,1,0:T(8,128)(2,1)} %gather_fusion.2), kind=kOutput, calls=%fused_computation.38 | convolution fusion | flops 268435456 | bytes 8388608 | tf_op jit(solution)/shard_map/kjab,kjcb->jac/dot_general | solution.py:55
  75.4 0.0 all-gather.3.cloned.1.call-update
  75.4 0.1 broadcast_compare_fusion
  75.5 20.2 %all-gather.3.cloned.1.call-done = f32[128,128,128]{2,1,0:T(8,128)} async-done(((f32[64,128,128]{2,1,0:T(8,128)}), f32[128,128,128]{2,1,0:T(8,128)}) %all-gather.3.cloned.1.call-update) | async-done | bytes 8388624 | tf_op jit(solution)/shard_map/all_gather | solution.py:9
  95.7 4.6 %reduce_sum.9 = bf16[64,128,128]{2,1,0:T(8,128)(2,1)S(1)} reduce(f32[2,64,128,128]{3,2,1,0:T(8,128)} %bitcast.26, f32[]{:T(128)} %constant.65.clone.1), dimensions={0}, to_apply=%region_3.4 | reduce | flops 1048576 | bytes 10485764 | tf_op jit(solution)/shard_map/reduce_sum | solution.py:10
  100.4 1.5 %and_select_fusion.1 = bf16[64,64,128]{2,1,0:T(8,128)(2,1)} fusion(bf16[64,128,128]{2,1,0:T(8,128)(2,1)S(1)} %reduce_sum.9, s32[]{:T(128)S(6)} %select_n.61, pred[64,128]{1,0:T(8,128)(4,1)S(1)} %get-tuple-element.14, pred[64,64]{1,0:T(8,128)(4,1)S(1)} %broadcast_compare_fusion), kind=kLoop, calls=%fused_computation.6 | loop fusion | flops 1048576 | bytes 2109444 | tf_op jit(solution)/shard_map/mul | solution.py:63
  (12 shorter events, 0.1 us)
Async XLA Ops:
  6.5 4.1 %copy-start = (bf16[1,8,128,128]{3,2,1,0:T(8,128)(2,1)S(1)}, bf16[1,8,128,128]{3,2,1,0:T(8,128)(2,1)}, u32[]{:S(2)}) copy-start(bf16[1,8,128,128]{3,2,1,0:T(8,128)(2,1)} %param.8) | copy-start | bytes 786436
  12.7 6.8 %copy-start.3 = (s32[128]{0:T(128)S(1)}, s32[128]{0:T(128)}, u32[]{:S(2)}) copy-start(s32[128]{0:T(128)} %param.9) | copy-start | bytes 1540
  12.7 7.8 %copy-start.1 = (s32[128]{0:T(128)S(1)}, s32[128]{0:T(128)}, u32[]{:S(2)}) copy-start(s32[128]{0:T(128)} %param.10) | copy-start | bytes 1540
  12.7 54.7 %all-to-all-start = ((bf16[1,16,4,128,128]{4,3,2,0,1:T(8,128)(2,1)}), bf16[1,16,4,128,128]{4,3,2,0,1:T(8,128)(2,1)S(1)}, u32[]{:S(2)}, u32[]{:S(2)}) async-start(bf16[1,16,4,128,128]{4,3,2,0,1:T(8,128)(2,1)} %bitcast.28), calls=%async_computation | async-start | bytes 4194304 | tf_op jit(solution)/shard_map/all_to_all | solution.py:53
  19.5 76.2 %all-gather.3.cloned.1.call-start = ((), (), s32[]{:S(2)}) async-start(), calls=%async_computation.1 | async-start | bytes 12582912 | tf_op jit(solution)/shard_map/all_gather | solution.py:9
  25.5 3.2 %copy-start.2 = (bf16[1,8,128,128]{3,2,1,0:T(8,128)(2,1)S(1)}, bf16[1,8,128,128]{3,2,1,0:T(8,128)(2,1)}, u32[]{:S(2)}) copy-start(bf16[1,8,128,128]{3,2,1,0:T(8,128)(2,1)} %param.7) | copy-start | bytes 786436
Sparse Core Ops, SparseCore 0:
  75.5 20.1 all-gather.2
